TPU v7x, 32 devices: a whole 2x2x4 slice. The times are simulated.
32 devices in a mesh: gx: 4 (over z), gy: 4 (over x, core), gz: 2 (over y).
Axes of the slice: x: 2, y: 2, z: 4, core: 2. Of those that a mesh axis runs over, the one named last changes fastest.
Arguments:
- activations: bfloat16 [1024, 8192], P('gy', 'gx'), may hold values from -0.5 to 0.5
- cotangent: bfloat16 [1024, 8192], P('gy', 'gx'), may hold values from -1.5 to 1.5
- gate_pre: bfloat16 [1024, 26624], P('gx', ('gy', 'gz')), may hold values from -6 to 6
- up_pre: bfloat16 [1024, 26624], P('gx', ('gy', 'gz')), may hold values from -6 to 6
- gate_weight: bfloat16 [8192, 26624], P('gx', ('gy', 'gz')), may hold values from -0.0625 to 0.0625
- up_weight: bfloat16 [8192, 26624], P('gx', ('gy', 'gz')), may hold values from -0.0625 to 0.0625
- down_weight: bfloat16 [26624, 8192], P(('gy', 'gz'), 'gx'), may hold values from -0.15625 to 0.15625
Outputs:
- input_grad: bfloat16 [1024, 8192], P('gy', 'gx')
- gate_grad: bfloat16 [8192, 26624], P('gx', ('gy', 'gz'))
- up_grad: bfloat16 [8192, 26624], P('gx', ('gy', 'gz'))
- down_grad: bfloat16 [26624, 8192], P(('gy', 'gz'), 'gx')
All inputs are finite; a program needn't handle non-finite values.
Results may differ from a plain program's by a relative error of at most 0.015.
Values may be sent and summed in bfloat16 or wider, within the bound.
A program may use at most 192 MiB of HBM per device.

v0:
```python
import jax
import jax.numpy as jnp
from jax import lax
from jax.sharding import PartitionSpec as P

over_rows = (((0,), (0,)), ((), ()))
over_cols = (((1,), (1,)), ((), ()))
BF = jnp.bfloat16
F32 = jnp.float32


def swiglu_grads(gate_in, up_in, grad_hidden):
    gate_val = gate_in.astype(F32)
    up_val = up_in.astype(F32)
    grad_hidden = grad_hidden.astype(F32)
    sigmoid = jax.nn.sigmoid(gate_val)
    hidden = (gate_val * sigmoid * up_val).astype(BF)
    grad_gate = (grad_hidden * up_val * sigmoid * (1.0 + gate_val * (1.0 - sigmoid))).astype(BF)
    grad_up = (grad_hidden * gate_val * sigmoid).astype(BF)
    return (hidden, grad_gate, grad_up)


def after(value, earlier):
    seen = earlier.reshape(-1)[0].astype(F32)
    return value + jnp.minimum(jnp.abs(seen), 0.0).astype(value.dtype)


def line_gather(block, axis, n):
    me = lax.axis_index(axis)
    right, left = ({}, {})
    from_left = from_right = block
    for s in range(1, n):
        from_left = lax.ppermute(from_left, axis, [(i, i + 1) for i in range(s - 1, n - 1)])
        from_right = lax.ppermute(from_right, axis, [(i, i - 1) for i in range(1, n - s + 1)])
        right[s], left[s] = (from_left, from_right)
    return [block] + [jnp.where(me >= r, right[r], left[n - r]) for r in range(1, n)]


def line_scatter(part, axis, n):
    right = left = None
    for t in range(1, n):
        to_right, to_left = (part(n - t), part(t))
        if right is not None:
            to_right = to_right + right.astype(F32)
            to_left = to_left + left.astype(F32)
        right = lax.ppermute(to_right.astype(BF), axis, [(i, i + 1) for i in range(min(t, n - 1))])
        left = lax.ppermute(to_left.astype(BF), axis, [(i, i - 1) for i in range(max(n - t, 1), n)])
    total = part(0)
    if right is not None:
        total = total + right.astype(F32) + left.astype(F32)
    return total


def pair_scatter(total, axis, n):
    me = lax.axis_index(axis)
    if n & n - 1:
        return lax.psum_scatter(total, axis, scatter_dimension=0, tiled=False)
    stride = 1
    while stride < n:
        pairs = total.reshape((total.shape[0] // 2, 2) + total.shape[1:])
        bit = me // stride % 2
        mine = lax.dynamic_index_in_dim(pairs, bit, 1, keepdims=False)
        theirs = lax.dynamic_index_in_dim(pairs, 1 - bit, 1, keepdims=False)
        got = lax.ppermute(theirs.astype(BF), axis, [(i, i ^ stride) for i in range(n)])
        total = mine + got.astype(F32)
        stride *= 2
    return total[0]


def chunks_of(width):
    tile = 256 if width % 256 == 0 else 64
    units = width // tile
    if width < 2048:
        return [(0, width)]
    sizes = [(units * 5 + 6) // 13, (units * 5 + 6) // 13]
    sizes.append(units - sum(sizes))
    out, at = ([], 0)
    for size in sizes:
        out.append((at * tile, size * tile))
        at += size
    return out


def shards(activations, cotangent, gate_pre, up_pre, gate_weight, up_weight, down_weight):
    n, ny, nz = (lax.axis_size("gx"), lax.axis_size("gy"), lax.axis_size("gz"))
    me = lax.axis_index("gx")
    rows = gate_pre.shape[0]
    tokens = n * rows
    width = gate_pre.shape[1]
    feats = activations.shape[1]
    cotangent_all = lax.all_gather(cotangent, "gy", axis=0, tiled=True)
    activations_all = lax.all_gather(activations, "gy", axis=0, tiled=True)

    def relative(whole):
        blocks = whole.reshape(n, rows, whole.shape[1])
        return jnp.concatenate(
            [
                lax.dynamic_index_in_dim(blocks, lax.rem(me - r + n, n), 0, keepdims=False)
                for r in range(n)
            ],
            axis=0,
        )

    cot = relative(cotangent_all)
    act = relative(activations_all)
    total = None
    gate_grad = jnp.zeros((feats, width), BF)
    up_grad = jnp.zeros((feats, width), BF)
    down_grad = jnp.zeros((width, feats), BF)
    chunks = chunks_of(width)
    partials = [
        lax.dot_general(
            cot,
            lax.slice_in_dim(down_weight, at, at + size, axis=0),
            over_cols,
            preferred_element_type=F32,
        ).reshape(n, rows, size)
        for at, size in chunks
    ]
    gates, sums = ([], [])
    for k, (at, size) in enumerate(chunks):
        gate = lax.slice_in_dim(gate_pre, at, at + size, axis=1)
        up = lax.slice_in_dim(up_pre, at, at + size, axis=1)
        if k == 1:
            gate, up = (after(gate, partials[1]), after(up, partials[1]))
        if k >= 2:
            gate, up = (after(gate, sums[k - 2]), after(up, sums[k - 2]))
        gates.append((line_gather(gate, "gx", n), line_gather(up, "gx", n)))

        def part(r, k=k):
            term = partials[k][(n - r) % n]
            return after(term, sums[k - 1]) if k and r in (1, n - 1) else term

        sums.append(line_scatter(part, "gx", n).astype(BF))
    for (at, size), (gate, up), own in zip(chunks, gates, sums):
        grad_hidden = line_gather(own, "gx", n)
        done = [swiglu_grads(*terms) for terms in zip(gate, up, grad_hidden)]
        hidden, grad_gate, grad_up = (jnp.concatenate(part, axis=0) for part in zip(*done))
        term = lax.dot_general(
            grad_gate,
            lax.slice_in_dim(gate_weight, at, at + size, axis=1),
            over_cols,
            preferred_element_type=F32,
        ) + lax.dot_general(
            grad_up,
            lax.slice_in_dim(up_weight, at, at + size, axis=1),
            over_cols,
            preferred_element_type=F32,
        )
        total = term if total is None else total + term
        down = lax.dot_general(hidden, cot, over_rows, preferred_element_type=F32).astype(BF)
        first = lax.dot_general(act, grad_gate, over_rows, preferred_element_type=F32).astype(BF)
        second = lax.dot_general(act, grad_up, over_rows, preferred_element_type=F32).astype(BF)
        down_grad = lax.dynamic_update_slice(down_grad, down, (at, 0))
        gate_grad = lax.dynamic_update_slice(gate_grad, first, (0, at))
        up_grad = lax.dynamic_update_slice(up_grad, second, (0, at))
    total = total.reshape(n, rows, feats)
    total = jnp.stack(
        [
            lax.dynamic_index_in_dim(total, lax.rem(me - j + n, n), 0, keepdims=False)
            for j in range(n)
        ]
    ).reshape(ny, tokens // ny, feats)
    share = pair_scatter(total, "gy", ny)
    if nz == 2:
        share = share + lax.ppermute(share.astype(BF), "gz", [(0, 1), (1, 0)]).astype(F32)
        input_grad = share.astype(BF)
    else:
        input_grad = lax.psum(share, "gz").astype(BF)
    return (input_grad, gate_grad, up_grad, down_grad)


def solution(mesh):
    in_specs = (
        P("gy", "gx"),
        P("gy", "gx"),
        P("gx", ("gy", "gz")),
        P("gx", ("gy", "gz")),
        P("gx", ("gy", "gz")),
        P("gx", ("gy", "gz")),
        P(("gy", "gz"), "gx"),
    )
    out_specs = (P("gy", "gx"), P("gx", ("gy", "gz")), P("gx", ("gy", "gz")), P(("gy", "gz"), "gx"))
    return jax.shard_map(shards, mesh=mesh, in_specs=in_specs, out_specs=out_specs, check_vma=False)
```

profile of v0, /device:TPU:0, one launch (start us, length us, event | category | flops | bytes accessed | tf_op | source)
XLA Modules:
  0.0 658.3 jit_solution(11141083498765120991)
XLA Ops:
  24.0 22.7 %all-gather.3.cloned.1.call-done = bf16[1024,2048]{1,0:T(8,128)(2,1)} async-done(((bf16[256,2048]{1,0:T(8,128)(2,1)}), bf16[1024,2048]{1,0:T(8,128)(2,1)}) %all-gather.3.cloned.1.call-update) | async-done | bytes 4194320 | tf_op jit(solution)/shard_map/all_gather | solution.py:91
  49.3 9.6 %fusion.13 = f32[1024,1280]{1,0:T(8,128)S(1)} fusion(bf16[3328,2048]{1,0:T(8,128)(2,1)} %param.13, bf16[256,2048]{1,0:T(8,128)(2,1)S(1)} %get-tuple-element.51, bf16[256,2048]{1,0:T(8,128)(2,1)S(1)} %get-tuple-element.52, bf16[256,2048]{1,0:T(8,128)(2,1)S(1)} %get-tuple-element.53, bf16[256,2048]{1,0:T(8,128)(2,1)S(1)} %get-tuple-element.50), kind=kOutput, calls=%fused_computation.21 | convolution fusion | flops 5385486336 | bytes 14680064 | tf_op jit(solution)/shard_map/dot_general | solution.py:112
  67.4 9.5 %collective-permute-done = bf16[256,1280]{1,0:T(8,128)(2,1)S(1)} collective-permute-done((bf16[256,1280]{1,0:T(8,128)(2,1)S(1)}, bf16[256,1280]{1,0:T(8,128)(2,1)S(1)}, u32[]{:S(2)}, u32[]{:S(2)}) %collective-permute-start) | collective-permute-done | bytes 655392 | tf_op jit(solution)/shard_map/ppermute | solution.py:46
  87.2 12.4 %collective-permute-done.16 = bf16[256,1280]{1,0:T(8,128)(2,1)} collective-permute-done((bf16[256,1280]{1,0:T(8,128)(2,1)}, bf16[256,1280]{1,0:T(8,128)(2,1)}, u32[]{:S(2)}, u32[]{:S(2)}) %collective-permute-start.16) | collective-permute-done | bytes 655392 | tf_op jit(solution)/shard_map/ppermute | solution.py:34
  119.2 12.1 %collective-permute-done.17 = bf16[256,1280]{1,0:T(8,128)(2,1)S(1)} collective-permute-done((bf16[256,1280]{1,0:T(8,128)(2,1)}, bf16[256,1280]{1,0:T(8,128)(2,1)S(1)}, u32[]{:S(2)}, u32[]{:S(2)}) %collective-permute-start.17) | collective-permute-done | bytes 655392 | tf_op jit(solution)/shard_map/ppermute | solution.py:34
  139.8 10.5 %fusion.7 = f32[1024,1280]{1,0:T(8,128)} fusion(bf16[3328,2048]{1,0:T(8,128)(2,1)} %param.13, bf16[256,2048]{1,0:T(8,128)(2,1)S(1)} %copy-done.64, bf16[256,2048]{1,0:T(8,128)(2,1)S(1)} %copy-done.69, bf16[256,2048]{1,0:T(8,128)(2,1)S(1)} %copy-done.74, bf16[256,2048]{1,0:T(8,128)(2,1)S(1)} %copy-done.59), kind=kOutput, calls=%fused_computation.15 | convolution fusion | flops 5385486336 | bytes 14680064 | tf_op jit(solution)/shard_map/dot_general | solution.py:112
  235.7 8.4 %convolution_convert_fusion.1 = bf16[1280,2048]{1,0:T(8,128)(2,1)S(1)} fusion(bf16[256,1280]{1,0:T(8,128)(2,1)S(1)} %copy-done.104, bf16[256,1280]{1,0:T(8,128)(2,1)S(1)} %copy-done.103, bf16[256,1280]{1,0:T(8,128)(2,1)} %get-tuple-element.22, bf16[256,1280]{1,0:T(8,128)(2,1)} %get-tuple-element.54, bf16[256,2048]{1,0:T(8,128)(2,1)} %copy-done.63, ...), kind=kOutput, calls=%fused_computation.4 | convolution fusion | flops 5398593536 | bytes 12058624 | tf_op jit(solution)/shard_map/dot_general | solution.py:151
  291.6 10.8 %collective-permute-done.8 = bf16[256,1280]{1,0:T(8,128)(2,1)} collective-permute-done((bf16[256,1280]{1,0:T(8,128)(2,1)}, bf16[256,1280]{1,0:T(8,128)(2,1)}, u32[]{:S(2)}, u32[]{:S(2)}) %collective-permute-start.8) | collective-permute-done | bytes 655392 | tf_op jit(solution)/shard_map/ppermute | solution.py:34
  306.9 9.5 %collective-permute-done.36 = bf16[256,1280]{1,0:T(8,128)(2,1)S(1)} collective-permute-done((bf16[256,1280]{1,0:T(8,128)(2,1)}, bf16[256,1280]{1,0:T(8,128)(2,1)S(1)}, u32[]{:S(2)}, u32[]{:S(2)}) %collective-permute-start.36) | collective-permute-done | bytes 655392 | tf_op jit(solution)/shard_map/ppermute | solution.py:34
  336.5 11.4 %collective-permute-done.37 = bf16[256,1280]{1,0:T(8,128)(2,1)S(1)} collective-permute-done((bf16[256,1280]{1,0:T(8,128)(2,1)S(1)}, bf16[256,1280]{1,0:T(8,128)(2,1)S(1)}, u32[]{:S(2)}, u32[]{:S(2)}) %collective-permute-start.37) | collective-permute-done | bytes 655392 | tf_op jit(solution)/shard_map/ppermute | solution.py:34
  350.2 11.7 %collective-permute-done.41 = bf16[256,1280]{1,0:T(8,128)(2,1)S(1)} collective-permute-done((bf16[256,1280]{1,0:T(8,128)(2,1)S(1)}, bf16[256,1280]{1,0:T(8,128)(2,1)S(1)}, u32[]{:S(2)}, u32[]{:S(2)}) %collective-permute-start.41) | collective-permute-done | bytes 655392 | tf_op jit(solution)/shard_map/ppermute | solution.py:34
  363.4 9.3 %fusion = bf16[3328,2048]{1,0:T(8,128)(2,1)} fusion(bf16[3328,2048]{1,0:T(8,128)(2,1)} %dynamic_update_slice.33, bf16[256,1280]{1,0:T(8,128)(2,1)S(1)} %get-tuple-element.20, bf16[256,1280]{1,0:T(8,128)(2,1)S(1)} %get-tuple-element.18, bf16[256,1280]{1,0:T(8,128)(2,1)S(1)} %get-tuple-element.16, bf16[256,1280]{1,0:T(8,128)(2,1)} %get-tuple-element.56, ...), kind=kOutput, calls=%fused_computation.3 | convolution fusion | flops 5398593536 | bytes 12058624 | tf_op jit(solution)/shard_map/dot_general | solution.py:151
  396.6 10.5 %fusion.11 = f32[1024,2048]{1,0:T(8,128)} fusion(bf16[2048,3328]{1,0:T(8,128)(2,1)} %param.11, bf16[256,1280]{1,0:T(8,128)(2,1)} %get-tuple-element.68, bf16[256,1280]{1,0:T(8,128)(2,1)} %get-tuple-element.66, bf16[256,1280]{1,0:T(8,128)(2,1)} %get-tuple-element.64, bf16[256,1280]{1,0:T(8,128)(2,1)} %get-tuple-element.55), kind=kOutput, calls=%fused_computation.19 | convolution fusion | flops 5379194880 | bytes 16252928 | tf_op jit(solution)/shard_map/dot_general | solution.py:139
  408.3 12.1 %fusion.9 = f32[1024,2048]{1,0:T(8,128)} fusion(bf16[2048,3328]{1,0:T(8,128)(2,1)} %param.12, bf16[256,1280]{1,0:T(8,128)(2,1)S(1)} %copy-done.89, bf16[256,1280]{1,0:T(8,128)(2,1)S(1)} %copy-done.87, bf16[256,1280]{1,0:T(8,128)(2,1)S(1)} %copy-done.90, bf16[256,1280]{1,0:T(8,128)(2,1)S(1)} %copy-done.86), kind=kOutput, calls=%fused_computation.17 | convolution fusion | flops 5379194880 | bytes 16252928 | tf_op jit(solution)/shard_map/dot_general | solution.py:144
  440.4 10.2 %collective-permute-start.50 = (bf16[256,768]{1,0:T(8,128)(2,1)S(1)}, bf16[256,768]{1,0:T(8,128)(2,1)S(1)}, u32[]{:S(2)}, u32[]{:S(2)}) collective-permute-start(bf16[256,768]{1,0:T(8,128)(2,1)S(1)} %get-tuple-element.59), channel_id=1, source_target_pairs={{0,8},{8,16},{16,24},{1,9},{9,17},{17,25},{2,10},{10,18},{18,26},{... | collective-permute-start | bytes 1179656 | tf_op jit(solution)/shard_map/ppermute | solution.py:46
  479.9 12.5 %fusion.5 = f32[1024,2048]{1,0:T(8,128)} fusion(bf16[2048,3328]{1,0:T(8,128)(2,1)} %param.11, bf16[256,1280]{1,0:T(8,128)(2,1)S(1)} %get-tuple-element.74, bf16[256,1280]{1,0:T(8,128)(2,1)S(1)} %get-tuple-element.72, bf16[256,1280]{1,0:T(8,128)(2,1)S(1)} %get-tuple-element.70, bf16[256,1280]{1,0:T(8,128)(2,1)S(1)} %fusion.64), kind=kOutput, calls=%fused_computation.13 | convolution fusion | flops 5379194880 | bytes 16252928 | tf_op jit(solution)/shard_map/dot_general | solution.py:139
  494.5 12.1 %fusion.3 = f32[1024,2048]{1,0:T(8,128)} fusion(bf16[2048,3328]{1,0:T(8,128)(2,1)} %param.12, bf16[256,1280]{1,0:T(8,128)(2,1)S(1)} %get-tuple-element.73, bf16[256,1280]{1,0:T(8,128)(2,1)S(1)} %get-tuple-element.71, bf16[256,1280]{1,0:T(8,128)(2,1)S(1)} %get-tuple-element.69, bf16[256,1280]{1,0:T(8,128)(2,1)S(1)} %copy-done.88), kind=kOutput, calls=%fused_computation.11 | convolution fusion | flops 5379194880 | bytes 16252928 | tf_op jit(solution)/shard_map/dot_general | solution.py:144
  524.8 9.5 %fusion.19 = f32[1024,2048]{1,0:T(8,128)} fusion(bf16[2048,3328]{1,0:T(8,128)(2,1)} %param.11, bf16[256,768]{1,0:T(8,128)(2,1)S(1)} %get-tuple-element.80, bf16[256,768]{1,0:T(8,128)(2,1)S(1)} %get-tuple-element.78, bf16[256,768]{1,0:T(8,128)(2,1)S(1)} %get-tuple-element.76, bf16[256,768]{1,0:T(8,128)(2,1)S(1)} %fusion.134), kind=kOutput, calls=%fused_computation.34 | convolution fusion | flops 3227516928 | bytes 13107200 | tf_op jit(solution)/shard_map/dot_general | solution.py:139
  534.4 18.9 %add_add_fusion = f32[1024,2048]{1,0:T(8,128)} fusion(f32[1024,2048]{1,0:T(8,128)} %fusion.19, f32[1024,2048]{1,0:T(8,128)} %fusion.5, f32[1024,2048]{1,0:T(8,128)} %fusion.3, f32[1024,2048]{1,0:T(8,128)} %fusion.11, f32[1024,2048]{1,0:T(8,128)} %fusion.9, bf16[2048,3328]{1,0:T(8,128)(2,1)} %param.12, bf16[256,768]{1,0:T(8,128)(2,1)S(1)} %get-tuple-element.79, ...), kind=kOutput, calls=%fused_computation.1 | convolution fusion | flops 3238002688 | bytes 55050240 | tf_op jit(solution)/shard_map/dot_general | solution.py:144
  558.6 11.2 %convolution_convert_fusion.3 = bf16[2048,1280]{1,0:T(8,128)(2,1)} fusion(bf16[256,1280]{1,0:T(8,128)(2,1)} %get-tuple-element.67, bf16[256,1280]{1,0:T(8,128)(2,1)} %get-tuple-element.65, bf16[256,1280]{1,0:T(8,128)(2,1)} %get-tuple-element.63, bf16[256,1280]{1,0:T(8,128)(2,1)} %get-tuple-element.30, bf16[256,2048]{1,0:T(8,128)(2,1)} %get-tuple-element.47, ...), kind=kOutput, calls=%fused_computation.7 | convolution fusion | flops 5398593536 | bytes 12058624 | tf_op jit(solution)/shard_map/dot_general | solution.py:153
  587.7 10.7 %fusion.2 = bf16[2048,3328]{1,0:T(8,128)(2,1)} fusion(bf16[2048,3328]{1,0:T(8,128)(2,1)} %dynamic_update_slice.27, bf16[256,1280]{1,0:T(8,128)(2,1)} %copy-done.98, bf16[256,1280]{1,0:T(8,128)(2,1)} %copy-done.95, bf16[256,1280]{1,0:T(8,128)(2,1)} %copy-done.99, bf16[256,1280]{1,0:T(8,128)(2,1)} %copy-done.91, bf16[256,2048]{1,0:T(8,128)(2,1)} %get-tuple-element.47, ...), kind=kOutput, calls=%fused_computation.9 | convolution fusion | flops 5398593536 | bytes 12058624 | tf_op jit(solution)/shard_map/dot_general | solution.py:152
  600.1 10.4 %fusion.1 = bf16[2048,3328]{1,0:T(8,128)(2,1)} fusion(bf16[2048,3328]{1,0:T(8,128)(2,1)} %dynamic_update_slice.30, bf16[256,1280]{1,0:T(8,128)(2,1)} %copy-done.96, bf16[256,1280]{1,0:T(8,128)(2,1)} %copy-done.93, bf16[256,1280]{1,0:T(8,128)(2,1)} %copy-done.97, bf16[256,1280]{1,0:T(8,128)(2,1)} %get-tuple-element.32, bf16[256,2048]{1,0:T(8,128)(2,1)S(1)} %copy-done.81, ...), kind=kOutput, calls=%fused_computation.6 | convolution fusion | flops 5398593536 | bytes 12058624 | tf_op jit(solution)/shard_map/dot_general | solution.py:153
  610.5 14.3 %collective-permute-done.73 = bf16[1,256,2048]{2,1,0:T(8,128)(2,1)S(1)} collective-permute-done((bf16[1,256,2048]{2,1,0:T(8,128)(2,1)S(1)}, bf16[1,256,2048]{2,1,0:T(8,128)(2,1)S(1)}, u32[]{:S(2)}, u32[]{:S(2)}) %collective-permute-start.73) | collective-permute-done | bytes 1048608 | tf_op jit(solution)/shard_map/ppermute | solution.py:64
  637.4 12.4 %collective-permute-done.74 = bf16[256,2048]{1,0:T(8,128)(2,1)S(1)} collective-permute-done((bf16[256,2048]{1,0:T(8,128)(2,1)S(1)}, bf16[256,2048]{1,0:T(8,128)(2,1)S(1)}, u32[]{:S(2)}, u32[]{:S(2)}) %collective-permute-start.74) | collective-permute-done | bytes 1048608 | tf_op jit(solution)/shard_map/ppermute | solution.py:166
  (457 shorter events, 357.3 us)
Async XLA Ops:
  7.2 39.6 %all-gather.3.cloned.1.call-start = ((), (), s32[]{:S(2)}) async-start(), calls=%async_computation | async-start | bytes 5242880 | tf_op jit(solution)/shard_map/all_gather | solution.py:91
  7.9 192.8 %all-gather.5.cloned.1.call-start = ((), (), s32[]{:S(2)}) async-start(), calls=%async_computation.1 | async-start | bytes 5242880 | tf_op jit(solution)/shard_map/all_gather | solution.py:92
  9.1 53.4 %collective-permute-start.10 = (bf16[256,1280]{1,0:T(8,128)(2,1)S(1)}, bf16[256,1280]{1,0:T(8,128)(2,1)S(1)}, u32[]{:S(2)}, u32[]{:S(2)}) collective-permute-start(bf16[256,1280]{1,0:T(8,128)(2,1)S(1)} %slice.125), channel_id=1, source_target_pairs={{0,8},{8,16},{16,24},{1,9},{9,17},{17,25},{2,10},{10,18},{18,26},{... | collective-permute-start | bytes 1966088 | tf_op jit(solution)/shard_map/ppermute | solution.py:33
  14.1 50.7 %collective-permute-start.11 = (bf16[256,1280]{1,0:T(8,128)(2,1)S(1)}, bf16[256,1280]{1,0:T(8,128)(2,1)S(1)}, u32[]{:S(2)}, u32[]{:S(2)}) collective-permute-start(bf16[256,1280]{1,0:T(8,128)(2,1)S(1)} %slice.125), channel_id=1, source_target_pairs={{8,0},{16,8},{24,16},{9,1},{17,9},{25,17},{10,2},{18,10},{26,18},{... | collective-permute-start | bytes 1966088 | tf_op jit(solution)/shard_map/ppermute | solution.py:34
  17.3 45.9 %collective-permute-start.14 = (bf16[256,1280]{1,0:T(8,128)(2,1)}, bf16[256,1280]{1,0:T(8,128)(2,1)}, u32[]{:S(2)}, u32[]{:S(2)}) collective-permute-start(bf16[256,1280]{1,0:T(8,128)(2,1)} %slice.126), channel_id=1, source_target_pairs={{0,8},{8,16},{16,24},{1,9},{9,17},{17,25},{2,10},{10,18},{18,26},{... | collective-permute-start | bytes 1966088 | tf_op jit(solution)/shard_map/ppermute | solution.py:33
  22.7 43.4 %collective-permute-start.15 = (bf16[256,1280]{1,0:T(8,128)(2,1)}, bf16[256,1280]{1,0:T(8,128)(2,1)}, u32[]{:S(2)}, u32[]{:S(2)}) collective-permute-start(bf16[256,1280]{1,0:T(8,128)(2,1)} %slice.126), channel_id=1, source_target_pairs={{8,0},{16,8},{24,16},{9,1},{17,9},{25,17},{10,2},{18,10},{26,18},{... | collective-permute-start | bytes 1966088 | tf_op jit(solution)/shard_map/ppermute | solution.py:34
  66.1 33.5 %collective-permute-start.16 = (bf16[256,1280]{1,0:T(8,128)(2,1)}, bf16[256,1280]{1,0:T(8,128)(2,1)}, u32[]{:S(2)}, u32[]{:S(2)}) collective-permute-start(bf16[256,1280]{1,0:T(8,128)(2,1)} %collective-permute-done.15), channel_id=1, source_target_pairs={{8,0},{16,8},{9,1},{17,9},{10,2},{18,10},{11,3},{19,11},{12,4},{20... | collective-permute-start | bytes 1966088 | tf_op jit(solution)/shard_map/ppermute | solution.py:34
  107.3 28.3 %collective-permute-start.4 = (bf16[256,1280]{1,0:T(8,128)(2,1)S(1)}, bf16[256,1280]{1,0:T(8,128)(2,1)S(1)}, u32[]{:S(2)}, u32[]{:S(2)}) collective-permute-start(bf16[256,1280]{1,0:T(8,128)(2,1)S(1)} %get-tuple-element.43), channel_id=1, source_target_pairs={{16,8},{24,16},{17,9},{25,17},{18,10},{26,18},{19,11},{27,19},{20,... | collective-permute-start | bytes 1966088 | tf_op jit(solution)/shard_map/ppermute | solution.py:47
  171.2 28.2 %collective-permute-start.59 = (bf16[256,768]{1,0:T(8,128)(2,1)S(1)}, bf16[256,768]{1,0:T(8,128)(2,1)}, u32[]{:S(2)}, u32[]{:S(2)}) collective-permute-start(bf16[256,768]{1,0:T(8,128)(2,1)S(1)} %get-tuple-element.5), channel_id=1, source_target_pairs={{8,0},{16,8},{24,16},{9,1},{17,9},{25,17},{10,2},{18,10},{26,18},{... | collective-permute-start | bytes 1179656 | tf_op jit(solution)/shard_map/ppermute | solution.py:34
  172.5 32.7 %collective-permute-start.62 = (bf16[256,768]{1,0:T(8,128)(2,1)S(1)}, bf16[256,768]{1,0:T(8,128)(2,1)}, u32[]{:S(2)}, u32[]{:S(2)}) collective-permute-start(bf16[256,768]{1,0:T(8,128)(2,1)S(1)} %get-tuple-element.6), channel_id=1, source_target_pairs={{0,8},{8,16},{16,24},{1,9},{9,17},{17,25},{2,10},{10,18},{18,26},{... | collective-permute-start | bytes 1179656 | tf_op jit(solution)/shard_map/ppermute | solution.py:33
  177.9 28.2 %collective-permute-start.63 = (bf16[256,768]{1,0:T(8,128)(2,1)S(1)}, bf16[256,768]{1,0:T(8,128)(2,1)}, u32[]{:S(2)}, u32[]{:S(2)}) collective-permute-start(bf16[256,768]{1,0:T(8,128)(2,1)S(1)} %get-tuple-element.6), channel_id=1, source_target_pairs={{8,0},{16,8},{24,16},{9,1},{17,9},{25,17},{10,2},{18,10},{26,18},{... | collective-permute-start | bytes 1179656 | tf_op jit(solution)/shard_map/ppermute | solution.py:34
  219.5 39.5 %collective-permute-start.6 = (bf16[256,1280]{1,0:T(8,128)(2,1)S(1)}, bf16[256,1280]{1,0:T(8,128)(2,1)}, u32[]{:S(2)}, u32[]{:S(2)}) collective-permute-start(bf16[256,1280]{1,0:T(8,128)(2,1)S(1)} %copy-done.5), channel_id=1, source_target_pairs={{0,8},{8,16},{16,24},{1,9},{9,17},{17,25},{2,10},{10,18},{18,26},{... | collective-permute-start | bytes 1966088 | tf_op jit(solution)/shard_map/ppermute | solution.py:33
  225.4 38.2 %collective-permute-start.7 = (bf16[256,1280]{1,0:T(8,128)(2,1)S(1)}, bf16[256,1280]{1,0:T(8,128)(2,1)}, u32[]{:S(2)}, u32[]{:S(2)}) collective-permute-start(bf16[256,1280]{1,0:T(8,128)(2,1)S(1)} %copy-done.5), channel_id=1, source_target_pairs={{8,0},{16,8},{24,16},{9,1},{17,9},{25,17},{10,2},{18,10},{26,18},{... | collective-permute-start | bytes 1966088 | tf_op jit(solution)/shard_map/ppermute | solution.py:34
  226.7 49.0 %collective-permute-start.27 = (bf16[256,1280]{1,0:T(8,128)(2,1)}, bf16[256,1280]{1,0:T(8,128)(2,1)}, u32[]{:S(2)}, u32[]{:S(2)}) collective-permute-start(bf16[256,1280]{1,0:T(8,128)(2,1)} %get-tuple-element.41), channel_id=1, source_target_pairs={{24,16},{25,17},{26,18},{27,19},{28,20},{29,21},{30,22},{31,23}} | collective-permute-start | bytes 1966088 | tf_op jit(solution)/shard_map/ppermute | solution.py:47
  280.0 46.9 %collective-permute-start.25 = (bf16[256,1280]{1,0:T(8,128)(2,1)S(1)}, bf16[256,1280]{1,0:T(8,128)(2,1)S(1)}, u32[]{:S(2)}, u32[]{:S(2)}) collective-permute-start(bf16[256,1280]{1,0:T(8,128)(2,1)S(1)} %copy-done.94), channel_id=1, source_target_pairs={{0,8},{8,16},{1,9},{9,17},{2,10},{10,18},{3,11},{11,19},{4,12},{12... | collective-permute-start | bytes 1966088 | tf_op jit(solution)/shard_map/ppermute | solution.py:46
  290.3 33.9 %collective-permute-start.40 = (bf16[256,1280]{1,0:T(8,128)(2,1)S(1)}, bf16[256,1280]{1,0:T(8,128)(2,1)S(1)}, u32[]{:S(2)}, u32[]{:S(2)}) collective-permute-start(bf16[256,1280]{1,0:T(8,128)(2,1)S(1)} %collective-permute-done.39), channel_id=1, source_target_pairs={{8,0},{16,8},{9,1},{17,9},{10,2},{18,10},{11,3},{19,11},{12,4},{20... | collective-permute-start | bytes 1966088 | tf_op jit(solution)/shard_map/ppermute | solution.py:34
  326.9 35.1 %collective-permute-start.41 = (bf16[256,1280]{1,0:T(8,128)(2,1)S(1)}, bf16[256,1280]{1,0:T(8,128)(2,1)S(1)}, u32[]{:S(2)}, u32[]{:S(2)}) collective-permute-start(bf16[256,1280]{1,0:T(8,128)(2,1)S(1)} %collective-permute-done.40), channel_id=1, source_target_pairs={{8,0},{9,1},{10,2},{11,3},{12,4},{13,5},{14,6},{15,7}} | collective-permute-start | bytes 1966088 | tf_op jit(solution)/shard_map/ppermute | solution.py:34
  328.2 44.6 %collective-permute-start.21 = (bf16[256,1280]{1,0:T(8,128)(2,1)}, bf16[256,1280]{1,0:T(8,128)(2,1)}, u32[]{:S(2)}, u32[]{:S(2)}) collective-permute-start(bf16[256,1280]{1,0:T(8,128)(2,1)} %collective-permute-done.18), channel_id=1, source_target_pairs={{16,24},{17,25},{18,26},{19,27},{20,28},{21,29},{22,30},{23,31}} | collective-permute-start | bytes 1966088 | tf_op jit(solution)/shard_map/ppermute | solution.py:33
  331.1 45.0 %collective-permute-start.9 = (bf16[256,1280]{1,0:T(8,128)(2,1)}, bf16[256,1280]{1,0:T(8,128)(2,1)}, u32[]{:S(2)}, u32[]{:S(2)}) collective-permute-start(bf16[256,1280]{1,0:T(8,128)(2,1)} %collective-permute-done.8), channel_id=1, source_target_pairs={{8,0},{9,1},{10,2},{11,3},{12,4},{13,5},{14,6},{15,7}} | collective-permute-start | bytes 1966088 | tf_op jit(solution)/shard_map/ppermute | solution.py:34
  332.4 50.8 %collective-permute-start.29 = (bf16[256,1280]{1,0:T(8,128)(2,1)}, bf16[256,1280]{1,0:T(8,128)(2,1)}, u32[]{:S(2)}, u32[]{:S(2)}) collective-permute-start(bf16[256,1280]{1,0:T(8,128)(2,1)} %get-tuple-element.39), channel_id=1, source_target_pairs={{8,0},{16,8},{24,16},{9,1},{17,9},{25,17},{10,2},{18,10},{26,18},{... | collective-permute-start | bytes 1966088 | tf_op jit(solution)/shard_map/ppermute | solution.py:47
  347.9 35.3 %collective-permute-start.26 = (bf16[256,1280]{1,0:T(8,128)(2,1)}, bf16[256,1280]{1,0:T(8,128)(2,1)}, u32[]{:S(2)}, u32[]{:S(2)}) collective-permute-start(bf16[256,1280]{1,0:T(8,128)(2,1)} %get-tuple-element.38), channel_id=1, source_target_pairs={{0,8},{8,16},{16,24},{1,9},{9,17},{17,25},{2,10},{10,18},{18,26},{... | collective-permute-start | bytes 1966088 | tf_op jit(solution)/shard_map/ppermute | solution.py:46
  439.0 29.3 %collective-permute-start.53 = (bf16[256,768]{1,0:T(8,128)(2,1)S(1)}, bf16[256,768]{1,0:T(8,128)(2,1)S(1)}, u32[]{:S(2)}, u32[]{:S(2)}) collective-permute-start(bf16[256,768]{1,0:T(8,128)(2,1)S(1)} %get-tuple-element.60), channel_id=1, source_target_pairs={{8,0},{16,8},{24,16},{9,1},{17,9},{25,17},{10,2},{18,10},{26,18},{... | collective-permute-start | bytes 1179656 | tf_op jit(solution)/shard_map/ppermute | solution.py:47
  440.4 27.8 %collective-permute-start.50 = (bf16[256,768]{1,0:T(8,128)(2,1)S(1)}, bf16[256,768]{1,0:T(8,128)(2,1)S(1)}, u32[]{:S(2)}, u32[]{:S(2)}) collective-permute-start(bf16[256,768]{1,0:T(8,128)(2,1)S(1)} %get-tuple-element.59), channel_id=1, source_target_pairs={{0,8},{8,16},{16,24},{1,9},{9,17},{17,25},{2,10},{10,18},{18,26},{... | collective-permute-start | bytes 1179656 | tf_op jit(solution)/shard_map/ppermute | solution.py:46
  558.5 39.9 %collective-permute-start.72 = (bf16[2,256,2048]{2,1,0:T(8,128)(2,1)S(1)}, bf16[2,256,2048]{2,1,0:T(8,128)(2,1)S(1)}, u32[]{:S(2)}, u32[]{:S(2)}) collective-permute-start(bf16[2,256,2048]{2,1,0:T(8,128)(2,1)S(1)} %fusion.37), channel_id=1, source_target_pairs={{0,2},{2,0},{4,6},{6,4},{1,3},{3,1},{5,7},{7,5},{8,10},{10,8},{12,... | collective-permute-start | bytes 6291464 | tf_op jit(solution)/shard_map/ppermute | solution.py:64
  (177 other events, 3323.6 us)
Sparse Core Ops, SparseCore 0:
  9.6 37.1 all-gather.2
  84.7 31.7 all-gather.4
where the time goes:
time: 668 us; the launch traced here: 658 us
  waiting for transfers between devices  201 us (30%)
  matrix products  175 us (26%)
  starting transfers between devices  147 us (22%)
  other arithmetic  66.6 us (10%)
  local copies, waits for them, and re-layouts  50.5 us (8%)
  between operations  18.3 us (3%)
    ppermute x27, waiting for transfers between devices, line_gather(): lax.ppermute(from_right, axis, [(i, i - 1) for i in range(1, n - s + 1)])  122 us
    ppermute x27, starting transfers between devices, line_gather(): lax.ppermute(from_left, axis, [(i, i + 1) for i in range(s - 1, n - 1)])  53 us
    ppermute x9, starting transfers between devices, line_scatter(): lax.ppermute(to_right.astype(BF), axis, [(i, i + 1) for i in range(min(t,...  45.5 us
    dot_general x3, matrix products, shards(): lax.dot_general(grad_up, lax.slice_in_dim(up_weight, at, at + size, axis=...  43 us
    ppermute x27, starting transfers between devices, line_gather(): lax.ppermute(from_right, axis, [(i, i - 1) for i in range(1, n - s + 1)])  35.5 us
    dot_general x3, matrix products, shards(): lax.dot_general(grad_gate, lax.slice_in_dim(gate_weight, at, at + size, a...  32.5 us
    dot_general x3, matrix products, shards(): lax.dot_general(act, grad_up, over_rows, preferred_element_type=F32)  26.9 us
    dot_general x3, matrix products, shards(): lax.dot_general(cot, lax.slice_in_dim(down_weight, at, at + size, axis=0)...  25.5 us
  transfers between devices with their start and end apart: 77, of which 25 were waited for; matrix products, arithmetic and copies ran while one was open for 37% of the time, Pallas kernels for 0%

commit v1 on v0

--- a/solution.py
+++ b/solution.py
@@ -88,8 +88,11 @@
     tokens = n * rows
     width = gate_pre.shape[1]
     feats = activations.shape[1]
-    cotangent_all = lax.all_gather(cotangent, "gy", axis=0, tiled=True)
-    activations_all = lax.all_gather(activations, "gy", axis=0, tiled=True)
+    cotangent_all, activations_all = jnp.split(
+        lax.all_gather(jnp.concatenate([cotangent, activations], axis=1), "gy", axis=0, tiled=True),
+        [cotangent.shape[1]],
+        axis=1,
+    )
 
     def relative(whole):
         blocks = whole.reshape(n, rows, whole.shape[1])

time: 668 us -> 691 us (1.034)
  waiting for transfers between devices: 201 us -> 233 us
  starting transfers between devices: 147 us -> 140 us
    all_gather x2 -> x1, waiting for transfers between devices: 22.8 us -> 45.2 us  [shards(): lax.all_gather(jnp.concatenate([cotangent, activations], axis=1), 'gy', a...]
  transfers between devices with their start and end apart: 77 -> 76, of which waited for: 25 -> 26; matrix products, arithmetic and copies ran while one was open for 37% -> 35% of each run, Pallas kernels for 0% -> 0%
where the time goes in v1:
time: 691 us; the launch traced here: 682 us
  waiting for transfers between devices  233 us (34%)
  matrix products  177 us (26%)
  starting transfers between devices  140 us (20%)
  other arithmetic  61.8 us (9%)
  local copies, waits for them, and re-layouts  51.4 us (7%)
  between operations  18.5 us (3%)
    ppermute x27, waiting for transfers between devices, line_gather(): lax.ppermute(from_right, axis, [(i, i - 1) for i in range(1, n - s + 1)])  127 us
    ppermute x27, starting transfers between devices, line_gather(): lax.ppermute(from_left, axis, [(i, i + 1) for i in range(s - 1, n - 1)])  50.8 us
    all_gather x1, waiting for transfers between devices, shards(): lax.all_gather(jnp.concatenate([cotangent, activations], axis=1), 'gy', a...  45.2 us
    dot_general x3, matrix products, shards(): lax.dot_general(grad_up, lax.slice_in_dim(up_weight, at, at + size, axis=...  43.1 us
    ppermute x9, starting transfers between devices, line_scatter(): lax.ppermute(to_right.astype(BF), axis, [(i, i + 1) for i in range(min(t,...  40.6 us
    ppermute x27, starting transfers between devices, line_gather(): lax.ppermute(from_right, axis, [(i, i - 1) for i in range(1, n - s + 1)])  35.4 us
    dot_general x3, matrix products, shards(): lax.dot_general(grad_gate, lax.slice_in_dim(gate_weight, at, at + size, a...  32.4 us
    dot_general x3, matrix products, shards(): lax.dot_general(cot, lax.slice_in_dim(down_weight, at, at + size, axis=0)...  27.1 us
  transfers between devices with their start and end apart: 76, of which 26 were waited for; matrix products, arithmetic and copies ran while one was open for 35% of the time, Pallas kernels for 0%

profile of v1, /device:TPU:0, one launch (start us, length us, event | category | flops | bytes accessed | tf_op | source)
XLA Modules:
  0.0 681.5 jit_solution(2609010984559637225)
XLA Ops:
  26.4 45.2 %all-gather.2.cloned.1.call-done = bf16[1024,4096]{1,0:T(8,128)(2,1)} async-done(((bf16[256,4096]{1,0:T(8,128)(2,1)}), bf16[1024,4096]{1,0:T(8,128)(2,1)}) %all-gather.2.cloned.1.call-update) | async-done | bytes 8388624 | tf_op jit(solution)/shard_map/all_gather | solution.py:92
  77.5 9.6 %fusion.13 = f32[1024,1280]{1,0:T(8,128)S(1)} fusion(bf16[3328,2048]{1,0:T(8,128)(2,1)} %param.13, bf16[256,2048]{1,0:T(8,128)(2,1)S(1)} %get-tuple-element.53, bf16[256,2048]{1,0:T(8,128)(2,1)S(1)} %get-tuple-element.54, bf16[256,2048]{1,0:T(8,128)(2,1)S(1)} %get-tuple-element.55, bf16[256,2048]{1,0:T(8,128)(2,1)S(1)} %get-tuple-element.52), kind=kOutput, calls=%fused_computation.21 | convolution fusion | flops 5385486336 | bytes 14680064 | tf_op jit(solution)/shard_map/dot_general | solution.py:115
  96.5 9.5 %collective-permute-done = bf16[256,1280]{1,0:T(8,128)(2,1)S(1)} collective-permute-done((bf16[256,1280]{1,0:T(8,128)(2,1)S(1)}, bf16[256,1280]{1,0:T(8,128)(2,1)S(1)}, u32[]{:S(2)}, u32[]{:S(2)}) %collective-permute-start) | collective-permute-done | bytes 655392 | tf_op jit(solution)/shard_map/ppermute | solution.py:46
  116.4 12.4 %collective-permute-done.16 = bf16[256,1280]{1,0:T(8,128)(2,1)} collective-permute-done((bf16[256,1280]{1,0:T(8,128)(2,1)}, bf16[256,1280]{1,0:T(8,128)(2,1)}, u32[]{:S(2)}, u32[]{:S(2)}) %collective-permute-start.16) | collective-permute-done | bytes 655392 | tf_op jit(solution)/shard_map/ppermute | solution.py:34
  148.5 12.1 %collective-permute-done.17 = bf16[256,1280]{1,0:T(8,128)(2,1)S(1)} collective-permute-done((bf16[256,1280]{1,0:T(8,128)(2,1)}, bf16[256,1280]{1,0:T(8,128)(2,1)S(1)}, u32[]{:S(2)}, u32[]{:S(2)}) %collective-permute-start.17) | collective-permute-done | bytes 655392 | tf_op jit(solution)/shard_map/ppermute | solution.py:34
  169.1 10.5 %fusion.7 = f32[1024,1280]{1,0:T(8,128)} fusion(bf16[3328,2048]{1,0:T(8,128)(2,1)} %param.13, bf16[256,2048]{1,0:T(8,128)(2,1)S(1)} %copy-done.63, bf16[256,2048]{1,0:T(8,128)(2,1)S(1)} %copy-done.68, bf16[256,2048]{1,0:T(8,128)(2,1)S(1)} %copy-done.73, bf16[256,2048]{1,0:T(8,128)(2,1)S(1)} %copy-done.59), kind=kOutput, calls=%fused_computation.15 | convolution fusion | flops 5385486336 | bytes 14680064 | tf_op jit(solution)/shard_map/dot_general | solution.py:115
  234.8 10.1 %collective-permute-done.34 = bf16[256,1280]{1,0:T(8,128)(2,1)S(1)} collective-permute-done((bf16[256,1280]{1,0:T(8,128)(2,1)S(1)}, bf16[256,1280]{1,0:T(8,128)(2,1)S(1)}, u32[]{:S(2)}, u32[]{:S(2)}) %collective-permute-start.34) | collective-permute-done | bytes 655392 | tf_op jit(solution)/shard_map/ppermute | solution.py:33
  318.5 10.7 %collective-permute-done.8 = bf16[256,1280]{1,0:T(8,128)(2,1)S(1)} collective-permute-done((bf16[256,1280]{1,0:T(8,128)(2,1)}, bf16[256,1280]{1,0:T(8,128)(2,1)S(1)}, u32[]{:S(2)}, u32[]{:S(2)}) %collective-permute-start.8) | collective-permute-done | bytes 655392 | tf_op jit(solution)/shard_map/ppermute | solution.py:34
  333.7 9.5 %collective-permute-done.36 = bf16[256,1280]{1,0:T(8,128)(2,1)S(1)} collective-permute-done((bf16[256,1280]{1,0:T(8,128)(2,1)S(1)}, bf16[256,1280]{1,0:T(8,128)(2,1)S(1)}, u32[]{:S(2)}, u32[]{:S(2)}) %collective-permute-start.36) | collective-permute-done | bytes 655392 | tf_op jit(solution)/shard_map/ppermute | solution.py:34
  363.0 12.0 %collective-permute-done.37 = bf16[256,1280]{1,0:T(8,128)(2,1)S(1)} collective-permute-done((bf16[256,1280]{1,0:T(8,128)(2,1)S(1)}, bf16[256,1280]{1,0:T(8,128)(2,1)S(1)}, u32[]{:S(2)}, u32[]{:S(2)}) %collective-permute-start.37) | collective-permute-done | bytes 655392 | tf_op jit(solution)/shard_map/ppermute | solution.py:34
  376.5 12.6 %collective-permute-done.41 = bf16[256,1280]{1,0:T(8,128)(2,1)S(1)} collective-permute-done((bf16[256,1280]{1,0:T(8,128)(2,1)S(1)}, bf16[256,1280]{1,0:T(8,128)(2,1)S(1)}, u32[]{:S(2)}, u32[]{:S(2)}) %collective-permute-start.41) | collective-permute-done | bytes 655392 | tf_op jit(solution)/shard_map/ppermute | solution.py:34
  390.8 9.8 %fusion = bf16[3328,2048]{1,0:T(8,128)(2,1)} fusion(bf16[3328,2048]{1,0:T(8,128)(2,1)} %dynamic_update_slice.33, bf16[256,1280]{1,0:T(8,128)(2,1)S(1)} %copy-done.102, bf16[256,1280]{1,0:T(8,128)(2,1)S(1)} %copy-done.101, bf16[256,1280]{1,0:T(8,128)(2,1)} %get-tuple-element.16, bf16[256,1280]{1,0:T(8,128)(2,1)} %get-tuple-element.58, ...), kind=kOutput, calls=%fused_computation.3 | convolution fusion | flops 5398593536 | bytes 12058624 | tf_op jit(solution)/shard_map/dot_general | solution.py:154
  420.0 10.5 %fusion.11 = f32[1024,2048]{1,0:T(8,128)} fusion(bf16[2048,3328]{1,0:T(8,128)(2,1)} %param.11, bf16[256,1280]{1,0:T(8,128)(2,1)} %get-tuple-element.70, bf16[256,1280]{1,0:T(8,128)(2,1)} %get-tuple-element.68, bf16[256,1280]{1,0:T(8,128)(2,1)} %get-tuple-element.66, bf16[256,1280]{1,0:T(8,128)(2,1)} %get-tuple-element.57), kind=kOutput, calls=%fused_computation.19 | convolution fusion | flops 5379194880 | bytes 16252928 | tf_op jit(solution)/shard_map/dot_general | solution.py:142
  431.6 12.1 %fusion.9 = f32[1024,2048]{1,0:T(8,128)} fusion(bf16[2048,3328]{1,0:T(8,128)(2,1)} %param.12, bf16[256,1280]{1,0:T(8,128)(2,1)S(1)} %copy-done.87, bf16[256,1280]{1,0:T(8,128)(2,1)S(1)} %copy-done.85, bf16[256,1280]{1,0:T(8,128)(2,1)S(1)} %copy-done.88, bf16[256,1280]{1,0:T(8,128)(2,1)S(1)} %copy-done.84), kind=kOutput, calls=%fused_computation.17 | convolution fusion | flops 5379194880 | bytes 16252928 | tf_op jit(solution)/shard_map/dot_general | solution.py:147
  463.8 10.3 %collective-permute-start.50 = (bf16[256,768]{1,0:T(8,128)(2,1)S(1)}, bf16[256,768]{1,0:T(8,128)(2,1)S(1)}, u32[]{:S(2)}, u32[]{:S(2)}) collective-permute-start(bf16[256,768]{1,0:T(8,128)(2,1)S(1)} %get-tuple-element.61), channel_id=1, source_target_pairs={{0,8},{8,16},{16,24},{1,9},{9,17},{17,25},{2,10},{10,18},{18,26},{... | collective-permute-start | bytes 1179656 | tf_op jit(solution)/shard_map/ppermute | solution.py:46
  502.1 12.4 %fusion.5 = f32[1024,2048]{1,0:T(8,128)} fusion(bf16[2048,3328]{1,0:T(8,128)(2,1)} %param.11, bf16[256,1280]{1,0:T(8,128)(2,1)S(1)} %get-tuple-element.76, bf16[256,1280]{1,0:T(8,128)(2,1)S(1)} %get-tuple-element.74, bf16[256,1280]{1,0:T(8,128)(2,1)S(1)} %get-tuple-element.72, bf16[256,1280]{1,0:T(8,128)(2,1)S(1)} %fusion.64), kind=kOutput, calls=%fused_computation.13 | convolution fusion | flops 5379194880 | bytes 16252928 | tf_op jit(solution)/shard_map/dot_general | solution.py:142
  516.7 12.1 %fusion.3 = f32[1024,2048]{1,0:T(8,128)} fusion(bf16[2048,3328]{1,0:T(8,128)(2,1)} %param.12, bf16[256,1280]{1,0:T(8,128)(2,1)S(1)} %get-tuple-element.75, bf16[256,1280]{1,0:T(8,128)(2,1)S(1)} %get-tuple-element.73, bf16[256,1280]{1,0:T(8,128)(2,1)S(1)} %get-tuple-element.71, bf16[256,1280]{1,0:T(8,128)(2,1)S(1)} %copy-done.86), kind=kOutput, calls=%fused_computation.11 | convolution fusion | flops 5379194880 | bytes 16252928 | tf_op jit(solution)/shard_map/dot_general | solution.py:147
  548.1 9.5 %fusion.19 = f32[1024,2048]{1,0:T(8,128)} fusion(bf16[2048,3328]{1,0:T(8,128)(2,1)} %param.11, bf16[256,768]{1,0:T(8,128)(2,1)S(1)} %get-tuple-element.82, bf16[256,768]{1,0:T(8,128)(2,1)S(1)} %get-tuple-element.80, bf16[256,768]{1,0:T(8,128)(2,1)S(1)} %get-tuple-element.78, bf16[256,768]{1,0:T(8,128)(2,1)S(1)} %fusion.134), kind=kOutput, calls=%fused_computation.34 | convolution fusion | flops 3227516928 | bytes 13107200 | tf_op jit(solution)/shard_map/dot_general | solution.py:142
  557.6 18.9 %add_add_fusion = f32[1024,2048]{1,0:T(8,128)} fusion(f32[1024,2048]{1,0:T(8,128)} %fusion.19, f32[1024,2048]{1,0:T(8,128)} %fusion.5, f32[1024,2048]{1,0:T(8,128)} %fusion.3, f32[1024,2048]{1,0:T(8,128)} %fusion.11, f32[1024,2048]{1,0:T(8,128)} %fusion.9, bf16[2048,3328]{1,0:T(8,128)(2,1)} %param.12, bf16[256,768]{1,0:T(8,128)(2,1)S(1)} %get-tuple-element.81, ...), kind=kOutput, calls=%fused_computation.1 | convolution fusion | flops 3238002688 | bytes 55050240 | tf_op jit(solution)/shard_map/dot_general | solution.py:147
  581.8 11.2 %convolution_convert_fusion.3 = bf16[2048,1280]{1,0:T(8,128)(2,1)} fusion(bf16[256,1280]{1,0:T(8,128)(2,1)} %get-tuple-element.69, bf16[256,1280]{1,0:T(8,128)(2,1)} %get-tuple-element.67, bf16[256,1280]{1,0:T(8,128)(2,1)} %get-tuple-element.65, bf16[256,1280]{1,0:T(8,128)(2,1)} %get-tuple-element.30, bf16[256,2048]{1,0:T(8,128)(2,1)} %get-tuple-element.49, ...), kind=kOutput, calls=%fused_computation.7 | convolution fusion | flops 5398593536 | bytes 12058624 | tf_op jit(solution)/shard_map/dot_general | solution.py:156
  610.9 10.7 %fusion.2 = bf16[2048,3328]{1,0:T(8,128)(2,1)} fusion(bf16[2048,3328]{1,0:T(8,128)(2,1)} %dynamic_update_slice.27, bf16[256,1280]{1,0:T(8,128)(2,1)} %copy-done.96, bf16[256,1280]{1,0:T(8,128)(2,1)} %copy-done.93, bf16[256,1280]{1,0:T(8,128)(2,1)} %copy-done.97, bf16[256,1280]{1,0:T(8,128)(2,1)} %copy-done.89, bf16[256,2048]{1,0:T(8,128)(2,1)} %get-tuple-element.49, ...), kind=kOutput, calls=%fused_computation.9 | convolution fusion | flops 5398593536 | bytes 12058624 | tf_op jit(solution)/shard_map/dot_general | solution.py:155
  623.3 10.4 %fusion.1 = bf16[2048,3328]{1,0:T(8,128)(2,1)} fusion(bf16[2048,3328]{1,0:T(8,128)(2,1)} %dynamic_update_slice.30, bf16[256,1280]{1,0:T(8,128)(2,1)} %copy-done.94, bf16[256,1280]{1,0:T(8,128)(2,1)} %copy-done.91, bf16[256,1280]{1,0:T(8,128)(2,1)} %copy-done.95, bf16[256,1280]{1,0:T(8,128)(2,1)} %get-tuple-element.32, bf16[256,2048]{1,0:T(8,128)(2,1)S(1)} %copy-done.79, ...), kind=kOutput, calls=%fused_computation.6 | convolution fusion | flops 5398593536 | bytes 12058624 | tf_op jit(solution)/shard_map/dot_general | solution.py:156
  633.7 14.3 %collective-permute-done.73 = bf16[1,256,2048]{2,1,0:T(8,128)(2,1)S(1)} collective-permute-done((bf16[1,256,2048]{2,1,0:T(8,128)(2,1)S(1)}, bf16[1,256,2048]{2,1,0:T(8,128)(2,1)S(1)}, u32[]{:S(2)}, u32[]{:S(2)}) %collective-permute-start.73) | collective-permute-done | bytes 1048608 | tf_op jit(solution)/shard_map/ppermute | solution.py:64
  660.6 12.4 %collective-permute-done.74 = bf16[256,2048]{1,0:T(8,128)(2,1)S(1)} collective-permute-done((bf16[256,2048]{1,0:T(8,128)(2,1)S(1)}, bf16[256,2048]{1,0:T(8,128)(2,1)S(1)}, u32[]{:S(2)}, u32[]{:S(2)}) %collective-permute-start.74) | collective-permute-done | bytes 1048608 | tf_op jit(solution)/shard_map/ppermute | solution.py:169
  (456 shorter events, 354.2 us)
Async XLA Ops:
  7.2 64.4 %all-gather.2.cloned.1.call-start = ((), (), s32[]{:S(2)}) async-start(), calls=%async_computation | async-start | bytes 10485760 | tf_op jit(solution)/shard_map/all_gather | solution.py:92
  12.5 79.1 %collective-permute-start.10 = (bf16[256,1280]{1,0:T(8,128)(2,1)}, bf16[256,1280]{1,0:T(8,128)(2,1)S(1)}, u32[]{:S(2)}, u32[]{:S(2)}) collective-permute-start(bf16[256,1280]{1,0:T(8,128)(2,1)} %slice.125), channel_id=1, source_target_pairs={{0,8},{8,16},{16,24},{1,9},{9,17},{17,25},{2,10},{10,18},{18,26},{... | collective-permute-start | bytes 1966088 | tf_op jit(solution)/shard_map/ppermute | solution.py:33
  17.4 76.5 %collective-permute-start.11 = (bf16[256,1280]{1,0:T(8,128)(2,1)}, bf16[256,1280]{1,0:T(8,128)(2,1)S(1)}, u32[]{:S(2)}, u32[]{:S(2)}) collective-permute-start(bf16[256,1280]{1,0:T(8,128)(2,1)} %slice.125), channel_id=1, source_target_pairs={{8,0},{16,8},{24,16},{9,1},{17,9},{25,17},{10,2},{18,10},{26,18},{... | collective-permute-start | bytes 1966088 | tf_op jit(solution)/shard_map/ppermute | solution.py:34
  19.7 72.7 %collective-permute-start.14 = (bf16[256,1280]{1,0:T(8,128)(2,1)}, bf16[256,1280]{1,0:T(8,128)(2,1)}, u32[]{:S(2)}, u32[]{:S(2)}) collective-permute-start(bf16[256,1280]{1,0:T(8,128)(2,1)} %slice.126), channel_id=1, source_target_pairs={{0,8},{8,16},{16,24},{1,9},{9,17},{17,25},{2,10},{10,18},{18,26},{... | collective-permute-start | bytes 1966088 | tf_op jit(solution)/shard_map/ppermute | solution.py:33
  25.1 70.2 %collective-permute-start.15 = (bf16[256,1280]{1,0:T(8,128)(2,1)}, bf16[256,1280]{1,0:T(8,128)(2,1)}, u32[]{:S(2)}, u32[]{:S(2)}) collective-permute-start(bf16[256,1280]{1,0:T(8,128)(2,1)} %slice.126), channel_id=1, source_target_pairs={{8,0},{16,8},{24,16},{9,1},{17,9},{25,17},{10,2},{18,10},{26,18},{... | collective-permute-start | bytes 1966088 | tf_op jit(solution)/shard_map/ppermute | solution.py:34
  95.2 33.5 %collective-permute-start.16 = (bf16[256,1280]{1,0:T(8,128)(2,1)}, bf16[256,1280]{1,0:T(8,128)(2,1)}, u32[]{:S(2)}, u32[]{:S(2)}) collective-permute-start(bf16[256,1280]{1,0:T(8,128)(2,1)} %collective-permute-done.15), channel_id=1, source_target_pairs={{8,0},{16,8},{9,1},{17,9},{10,2},{18,10},{11,3},{19,11},{12,4},{20... | collective-permute-start | bytes 1966088 | tf_op jit(solution)/shard_map/ppermute | solution.py:34
  106.0 27.0 %collective-permute-start.3 = (bf16[256,1280]{1,0:T(8,128)(2,1)}, bf16[256,1280]{1,0:T(8,128)(2,1)}, u32[]{:S(2)}, u32[]{:S(2)}) collective-permute-start(bf16[256,1280]{1,0:T(8,128)(2,1)} %get-tuple-element.47), channel_id=1, source_target_pairs={{24,16},{25,17},{26,18},{27,19},{28,20},{29,21},{30,22},{31,23}} | collective-permute-start | bytes 1966088 | tf_op jit(solution)/shard_map/ppermute | solution.py:47
  133.0 27.7 %collective-permute-start.17 = (bf16[256,1280]{1,0:T(8,128)(2,1)}, bf16[256,1280]{1,0:T(8,128)(2,1)S(1)}, u32[]{:S(2)}, u32[]{:S(2)}) collective-permute-start(bf16[256,1280]{1,0:T(8,128)(2,1)} %collective-permute-done.16), channel_id=1, source_target_pairs={{8,0},{9,1},{10,2},{11,3},{12,4},{13,5},{14,6},{15,7}} | collective-permute-start | bytes 1966088 | tf_op jit(solution)/shard_map/ppermute | solution.py:34
  137.4 27.6 %collective-permute-start.4 = (bf16[256,1280]{1,0:T(8,128)(2,1)S(1)}, bf16[256,1280]{1,0:T(8,128)(2,1)S(1)}, u32[]{:S(2)}, u32[]{:S(2)}) collective-permute-start(bf16[256,1280]{1,0:T(8,128)(2,1)S(1)} %get-tuple-element.45), channel_id=1, source_target_pairs={{16,8},{24,16},{17,9},{25,17},{18,10},{26,18},{19,11},{27,19},{20,... | collective-permute-start | bytes 1966088 | tf_op jit(solution)/shard_map/ppermute | solution.py:47
  203.6 27.3 %collective-permute-start.62 = (bf16[256,768]{1,0:T(8,128)(2,1)S(1)}, bf16[256,768]{1,0:T(8,128)(2,1)S(1)}, u32[]{:S(2)}, u32[]{:S(2)}) collective-permute-start(bf16[256,768]{1,0:T(8,128)(2,1)S(1)} %get-tuple-element.6), channel_id=1, source_target_pairs={{0,8},{8,16},{16,24},{1,9},{9,17},{17,25},{2,10},{10,18},{18,26},{... | collective-permute-start | bytes 1179656 | tf_op jit(solution)/shard_map/ppermute | solution.py:33
  247.6 38.0 %collective-permute-start.6 = (bf16[256,1280]{1,0:T(8,128)(2,1)S(1)}, bf16[256,1280]{1,0:T(8,128)(2,1)}, u32[]{:S(2)}, u32[]{:S(2)}) collective-permute-start(bf16[256,1280]{1,0:T(8,128)(2,1)S(1)} %get-tuple-element.31), channel_id=1, source_target_pairs={{0,8},{8,16},{16,24},{1,9},{9,17},{17,25},{2,10},{10,18},{18,26},{... | collective-permute-start | bytes 1966088 | tf_op jit(solution)/shard_map/ppermute | solution.py:33
  253.4 36.8 %collective-permute-start.7 = (bf16[256,1280]{1,0:T(8,128)(2,1)S(1)}, bf16[256,1280]{1,0:T(8,128)(2,1)}, u32[]{:S(2)}, u32[]{:S(2)}) collective-permute-start(bf16[256,1280]{1,0:T(8,128)(2,1)S(1)} %get-tuple-element.31), channel_id=1, source_target_pairs={{8,0},{16,8},{24,16},{9,1},{17,9},{25,17},{10,2},{18,10},{26,18},{... | collective-permute-start | bytes 1966088 | tf_op jit(solution)/shard_map/ppermute | solution.py:34
  254.7 47.9 %collective-permute-start.27 = (bf16[256,1280]{1,0:T(8,128)(2,1)}, bf16[256,1280]{1,0:T(8,128)(2,1)}, u32[]{:S(2)}, u32[]{:S(2)}) collective-permute-start(bf16[256,1280]{1,0:T(8,128)(2,1)} %get-tuple-element.43), channel_id=1, source_target_pairs={{24,16},{25,17},{26,18},{27,19},{28,20},{29,21},{30,22},{31,23}} | collective-permute-start | bytes 1966088 | tf_op jit(solution)/shard_map/ppermute | solution.py:47
  306.8 47.3 %collective-permute-start.25 = (bf16[256,1280]{1,0:T(8,128)(2,1)S(1)}, bf16[256,1280]{1,0:T(8,128)(2,1)S(1)}, u32[]{:S(2)}, u32[]{:S(2)}) collective-permute-start(bf16[256,1280]{1,0:T(8,128)(2,1)S(1)} %copy-done.92), channel_id=1, source_target_pairs={{0,8},{8,16},{1,9},{9,17},{2,10},{10,18},{3,11},{11,19},{4,12},{12... | collective-permute-start | bytes 1966088 | tf_op jit(solution)/shard_map/ppermute | solution.py:46
  315.9 27.4 %collective-permute-start.36 = (bf16[256,1280]{1,0:T(8,128)(2,1)S(1)}, bf16[256,1280]{1,0:T(8,128)(2,1)S(1)}, u32[]{:S(2)}, u32[]{:S(2)}) collective-permute-start(bf16[256,1280]{1,0:T(8,128)(2,1)S(1)} %collective-permute-done.35), channel_id=1, source_target_pairs={{8,0},{16,8},{9,1},{17,9},{10,2},{18,10},{11,3},{19,11},{12,4},{20... | collective-permute-start | bytes 1966088 | tf_op jit(solution)/shard_map/ppermute | solution.py:34
  317.2 34.0 %collective-permute-start.40 = (bf16[256,1280]{1,0:T(8,128)(2,1)S(1)}, bf16[256,1280]{1,0:T(8,128)(2,1)S(1)}, u32[]{:S(2)}, u32[]{:S(2)}) collective-permute-start(bf16[256,1280]{1,0:T(8,128)(2,1)S(1)} %collective-permute-done.39), channel_id=1, source_target_pairs={{8,0},{16,8},{9,1},{17,9},{10,2},{18,10},{11,3},{19,11},{12,4},{20... | collective-permute-start | bytes 1966088 | tf_op jit(solution)/shard_map/ppermute | solution.py:34
  354.1 34.9 %collective-permute-start.41 = (bf16[256,1280]{1,0:T(8,128)(2,1)S(1)}, bf16[256,1280]{1,0:T(8,128)(2,1)S(1)}, u32[]{:S(2)}, u32[]{:S(2)}) collective-permute-start(bf16[256,1280]{1,0:T(8,128)(2,1)S(1)} %collective-permute-done.40), channel_id=1, source_target_pairs={{8,0},{9,1},{10,2},{11,3},{12,4},{13,5},{14,6},{15,7}} | collective-permute-start | bytes 1966088 | tf_op jit(solution)/shard_map/ppermute | solution.py:34
  355.4 45.2 %collective-permute-start.21 = (bf16[256,1280]{1,0:T(8,128)(2,1)}, bf16[256,1280]{1,0:T(8,128)(2,1)}, u32[]{:S(2)}, u32[]{:S(2)}) collective-permute-start(bf16[256,1280]{1,0:T(8,128)(2,1)} %collective-permute-done.18), channel_id=1, source_target_pairs={{16,24},{17,25},{18,26},{19,27},{20,28},{21,29},{22,30},{23,31}} | collective-permute-start | bytes 1966088 | tf_op jit(solution)/shard_map/ppermute | solution.py:33
  358.4 45.4 %collective-permute-start.9 = (bf16[256,1280]{1,0:T(8,128)(2,1)S(1)}, bf16[256,1280]{1,0:T(8,128)(2,1)}, u32[]{:S(2)}, u32[]{:S(2)}) collective-permute-start(bf16[256,1280]{1,0:T(8,128)(2,1)S(1)} %collective-permute-done.8), channel_id=1, source_target_pairs={{8,0},{9,1},{10,2},{11,3},{12,4},{13,5},{14,6},{15,7}} | collective-permute-start | bytes 1966088 | tf_op jit(solution)/shard_map/ppermute | solution.py:34
  359.8 51.8 %collective-permute-start.29 = (bf16[256,1280]{1,0:T(8,128)(2,1)}, bf16[256,1280]{1,0:T(8,128)(2,1)S(1)}, u32[]{:S(2)}, u32[]{:S(2)}) collective-permute-start(bf16[256,1280]{1,0:T(8,128)(2,1)} %get-tuple-element.41), channel_id=1, source_target_pairs={{8,0},{16,8},{24,16},{9,1},{17,9},{25,17},{10,2},{18,10},{26,18},{... | collective-permute-start | bytes 1966088 | tf_op jit(solution)/shard_map/ppermute | solution.py:47
  375.0 36.5 %collective-permute-start.26 = (bf16[256,1280]{1,0:T(8,128)(2,1)}, bf16[256,1280]{1,0:T(8,128)(2,1)S(1)}, u32[]{:S(2)}, u32[]{:S(2)}) collective-permute-start(bf16[256,1280]{1,0:T(8,128)(2,1)} %get-tuple-element.40), channel_id=1, source_target_pairs={{0,8},{8,16},{16,24},{1,9},{9,17},{17,25},{2,10},{10,18},{18,26},{... | collective-permute-start | bytes 1966088 | tf_op jit(solution)/shard_map/ppermute | solution.py:46
  462.3 29.0 %collective-permute-start.53 = (bf16[256,768]{1,0:T(8,128)(2,1)S(1)}, bf16[256,768]{1,0:T(8,128)(2,1)S(1)}, u32[]{:S(2)}, u32[]{:S(2)}) collective-permute-start(bf16[256,768]{1,0:T(8,128)(2,1)S(1)} %get-tuple-element.62), channel_id=1, source_target_pairs={{8,0},{16,8},{24,16},{9,1},{17,9},{25,17},{10,2},{18,10},{26,18},{... | collective-permute-start | bytes 1179656 | tf_op jit(solution)/shard_map/ppermute | solution.py:47
  463.8 27.5 %collective-permute-start.50 = (bf16[256,768]{1,0:T(8,128)(2,1)S(1)}, bf16[256,768]{1,0:T(8,128)(2,1)S(1)}, u32[]{:S(2)}, u32[]{:S(2)}) collective-permute-start(bf16[256,768]{1,0:T(8,128)(2,1)S(1)} %get-tuple-element.61), channel_id=1, source_target_pairs={{0,8},{8,16},{16,24},{1,9},{9,17},{17,25},{2,10},{10,18},{18,26},{... | collective-permute-start | bytes 1179656 | tf_op jit(solution)/shard_map/ppermute | solution.py:46
  581.7 39.9 %collective-permute-start.72 = (bf16[2,256,2048]{2,1,0:T(8,128)(2,1)S(1)}, bf16[2,256,2048]{2,1,0:T(8,128)(2,1)S(1)}, u32[]{:S(2)}, u32[]{:S(2)}) collective-permute-start(bf16[2,256,2048]{2,1,0:T(8,128)(2,1)S(1)} %fusion.37), channel_id=1, source_target_pairs={{0,2},{2,0},{4,6},{6,4},{1,3},{3,1},{5,7},{7,5},{8,10},{10,8},{12,... | collective-permute-start | bytes 6291464 | tf_op jit(solution)/shard_map/ppermute | solution.py:64
  (176 other events, 3392.0 us)
Sparse Core Ops, SparseCore 0:
  10.6 60.9 all-gather.1
